TPU v7x, 32 devices: a whole 2x2x4 slice. The times are simulated.
32 devices in a mesh: path: 8 (over z, core), fsdp: 4 (over y, x).
Axes of the slice: x: 2, y: 2, z: 4, core: 2. Of those that a mesh axis runs over, the one named last changes fastest.
Arguments:
- path_delta: bfloat16 [8, 4, 128, 4096], P('path', None, 'fsdp'), may hold values from -20 to 20
- feedback: float32 [8, 4, 128, 4096], P('path', None, 'fsdp'), may hold values from -4 to 4
- global_params: float32 [4, 2, 128, 4096], P(None, None, 'fsdp', 'path'), may hold values from -0.09375 to 0.09375
- momentum: float32 [4, 2, 128, 4096], P(None, None, 'fsdp', 'path'), may hold values from -2 to 2
- routes: int32 [8, 4], replicated, may hold values from 0 to 1
- token_counts: int32 [8, 4], replicated, may hold values from 1 to 16
- skip_flags: int32 [4, 2], replicated, may hold values from 0 to 1, as said below
Outputs:
- feedback_next: float32 [8, 4, 128, 4096], P('path', None, 'fsdp')
- momentum_next: float32 [4, 2, 128, 4096], P(None, None, 'fsdp', 'path')
- params_next: float32 [4, 2, 128, 4096], P(None, None, 'fsdp', 'path')
- path_params: bfloat16 [8, 4, 128, 4096], P('path', None, 'fsdp')
Inputs may be any that keep to these rules, and one draw needn't show every extreme that they name: `skip_flags`: at most one of the two modules of a level skips.
All inputs are finite; a program needn't handle non-finite values.
Results may differ from a plain program's by a relative error of at most 0.012.
Values may be sent and summed in bfloat16 or wider, within the bound.
A program may use at most 64 MiB of HBM per device.

v0:
```python
import jax
import jax.numpy as jnp
from jax import lax
from jax.sharding import PartitionSpec as P

clip_rms = 0.2
outer_rate = 0.7
momentum_coef = 0.9
epsilon_sq = 1e-06


def on_device(path_delta, feedback, global_params, momentum, routes, token_counts, skip_flags):
    own_index = lax.axis_index("path")
    counts = token_counts.astype(jnp.float32)
    same = (routes[:, None, :] == routes[None, :, :]).astype(jnp.float32)
    denom = jnp.sum(same * counts[None, :, :], axis=1)
    weight = counts / denom
    skipped_path = jnp.where(routes == 1, skip_flags[None, :, 1], skip_flags[None, :, 0])
    live = (1 - skipped_path).astype(jnp.float32)
    own_weight = lax.dynamic_slice_in_dim(weight, own_index, 1, 0)[0]
    own_live = lax.dynamic_slice_in_dim(live, own_index, 1, 0)[0]
    own_route = lax.dynamic_slice_in_dim(routes, own_index, 1, 0)[0]
    corrected = path_delta[0].astype(jnp.float32) + feedback[0]
    scaled = (own_weight[:, None, None] * corrected).astype(jnp.bfloat16)
    sent = jnp.where(own_live[:, None, None] > 0, scaled, jnp.zeros_like(scaled))
    feedback_next = corrected - own_live[:, None, None] * (
        sent.astype(jnp.float32) / own_weight[:, None, None]
    )
    own_hot = (own_route[:, None] == jnp.arange(2, dtype=jnp.int32)[None, :]).astype(jnp.float32)
    terms = own_hot[:, :, None, None] * sent.astype(jnp.float32)[:, None]
    average = lax.psum_scatter(
        terms.astype(jnp.bfloat16), "path", scatter_dimension=3, tiled=True
    ).astype(jnp.float32)
    local_sq = jnp.sum(average * average, axis=(2, 3))
    total_sq = lax.psum(local_sq, ("path", "fsdp"))
    entries = average.shape[2] * average.shape[3] * lax.axis_size("path") * lax.axis_size("fsdp")
    factor = jnp.minimum(1.0, clip_rms / jnp.sqrt(total_sq / entries + epsilon_sq))
    clipped = factor[:, :, None, None] * average
    skipped = (skip_flags > 0)[:, :, None, None]
    momentum_next = jnp.where(skipped, momentum, momentum_coef * momentum + clipped)
    params_next = jnp.where(
        skipped,
        global_params,
        global_params - outer_rate * (clipped + momentum_coef * momentum_next),
    )
    narrow = params_next.astype(jnp.bfloat16)
    outgoing = jnp.where((routes == 1)[:, :, None, None], narrow[None, :, 1], narrow[None, :, 0])
    returned = lax.all_to_all(outgoing, "path", split_axis=0, concat_axis=3, tiled=True)
    return (feedback_next[None], momentum_next, params_next, returned)


def solution(mesh):
    return jax.shard_map(
        on_device,
        mesh=mesh,
        in_specs=(
            P("path", None, "fsdp", None),
            P("path", None, "fsdp", None),
            P(None, None, "fsdp", "path"),
            P(None, None, "fsdp", "path"),
            P(),
            P(),
            P(),
        ),
        out_specs=(
            P("path", None, "fsdp", None),
            P(None, None, "fsdp", "path"),
            P(None, None, "fsdp", "path"),
            P("path", None, "fsdp", None),
        ),
        check_vma=False,
    )
```

profile of v0, /device:TPU:0, one launch (start us, length us, event | category | flops | bytes accessed | tf_op | source)
XLA Modules:
  0.0 136.3 jit_solution(1709357491064695534)
XLA Ops:
  7.2 0.0 reduce-scatter.2.cloned.1.call-start
  7.2 0.8 slice_bitcast_fusion.3
  8.0 0.7 convert_element_type.55
  8.7 0.9 select_reduce_fusion
  9.6 0.7 convert_divide_fusion
  10.3 0.9 dynamic-slice_reduce_fusion
  11.1 0.8 subtract_convert_fusion
  11.9 0.2 dynamic-slice_reduce_fusion.1
  12.1 0.1 fusion.9
  12.2 2.3 %fusion.3 = f32[4,32,4096]{2,1,0:T(8,128)S(1)} fusion(f32[1,4,32,4096]{3,2,1,0:T(8,128)} %param.8, bf16[1,4,32,4096]{3,2,1,0:T(8,128)(2,1)} %param.7, f32[4]{0:T(128)S(1)} %get-tuple-element.13, pred[4]{0:T(512)(128)(4,1)S(1)} %broadcast_compare_fusion.2), kind=kLoop, calls=%fused_computation.8 | loop fusion | flops 3145728 | bytes 5242900 | tf_op jit(solution)/shard_map/convert_element_type | solution.py:27
  14.5 1.7 %multiply_convert_fusion = bf16[4,2,32,4096]{3,2,1,0:T(8,128)(2,1)} fusion(f32[4,32,4096]{2,1,0:T(8,128)S(1)} %fusion.3, f32[4,2]{1,0:T(4,128)S(1)} %fusion.9), kind=kLoop, calls=%fused_computation | loop fusion | flops 2097152 | bytes 4194336 | tf_op jit(solution)/shard_map/convert_element_type | solution.py:32
  16.2 0.0 copy-start.3
  16.2 0.0 copy-start.1
  16.2 0.0 copy-start.2
  16.2 0.0 reduce-scatter.2.cloned.1.call-update
  16.2 0.6 copy-done.3
  16.9 0.1 copy.29
  17.0 38.2 %reduce-scatter.2.cloned.1.call-done = bf16[4,2,32,512]{3,2,1,0:T(8,128)(2,1)} async-done(((bf16[4,2,32,4096]{3,2,1,0:T(8,128)(2,1)}), bf16[4,2,32,512]{3,2,1,0:T(8,128)(2,1)}) %reduce-scatter.2.cloned.1.call-update) | async-done | bytes 262160 | tf_op jit(solution)/shard_map/reduce_scatter | solution.py:31
  55.1 1.1 fusion.8
  56.2 0.1 copy.30
  56.3 37.9 %psum.7 = f32[4,2]{1,0:T(4,128)S(1)} all-reduce(f32[4,2]{1,0:T(4,128)S(1)} %fusion.8), channel_id=1, replica_groups=mesh['path'=8,'fsdp'=4] {'path','fsdp'}, use_global_device_ids=true, to_apply=%region_3.4 | all-reduce | flops 8 | bytes 64 | tf_op jit(solution)/shard_map/psum | solution.py:35
  94.2 0.0 copy-done.1
  94.2 0.0 copy-done.2
  94.2 2.2 %fusion.10 = (bf16[4,2,32,512]{3,2,1,0:T(8,128)(2,1)S(1)}, f32[4,2,32,512]{3,2,1,0:T(8,128)}, f32[4,2,32,512]{3,2,1,0:T(8,128)}) fusion(f32[4,2,32,512]{3,2,1,0:T(8,128)S(1)} %copy-done.1, bf16[4,2,32,512]{3,2,1,0:T(8,128)(2,1)} %reduce-scatter.2.cloned.1.call-done, f32[4,2]{1,0:T(4,128)S(1)} %multiply_minimum_fusion, pred[4,2]{1,0:T(4,128)(4,1)S(1)} %copy.29, ...), kind=kLoop, calls=%fused_computation.34 | loop fusion | flops 1441792 | bytes 2621480 | tf_op jit(solution)/shard_map/convert_element_type | solution.py:46
  96.5 0.0 copy-start
  96.5 1.1 broadcast_select_fusion
  97.6 4.2 %all-to-all-start = ((bf16[8,4,32,512]{3,2,1,0:T(8,128)(2,1)}), bf16[8,4,32,512]{3,2,1,0:T(8,128)(2,1)S(1)}, u32[]{:S(2)}, u32[]{:S(2)}) async-start(bf16[8,4,32,512]{3,2,1,0:T(8,128)(2,1)} %broadcast_select_fusion), calls=%async_computation.1 | async-start | bytes 2097152 | tf_op jit(solution)/shard_map/all_to_all | solution.py:48
  101.8 0.0 copy-done
  101.8 3.1 %multiply_subtract_fusion = f32[1,4,32,4096]{3,2,1,0:T(8,128)} fusion(f32[1,4,32,4096]{3,2,1,0:T(8,128)S(1)} %copy-done, bf16[1,4,32,4096]{3,2,1,0:T(8,128)(2,1)} %param.7, f32[4]{0:T(128)S(1)} %get-tuple-element.13, f32[4]{0:T(128)S(1)} %get-tuple-element.14, pred[4]{0:T(512)(128)(4,1)S(1)} %broadcast_compare_fusion.2), kind=kLoop, calls=%fused_computation.3 | loop fusion | flops 4718592 | bytes 5242916 | tf_op jit(solution)/shard_map/sub | solution.py:26
  104.9 23.5 %all-to-all-done = bf16[8,4,32,512]{3,2,1,0:T(8,128)(2,1)S(1)} async-done(((bf16[8,4,32,512]{3,2,1,0:T(8,128)(2,1)}), bf16[8,4,32,512]{3,2,1,0:T(8,128)(2,1)S(1)}, u32[]{:S(2)}, u32[]{:S(2)}) %all-to-all-start) | async-done | bytes 1048608 | tf_op jit(solution)/shard_map/all_to_all | solution.py:48
  128.4 1.1 copy.32
  (4 shorter events, 0.0 us)
Async XLA Ops:
  7.2 48.0 %reduce-scatter.2.cloned.1.call-start = ((), (), s32[]{:S(2)}) async-start(), calls=%async_computation.2 | async-start | bytes 2359296 | tf_op jit(solution)/shard_map/reduce_scatter | solution.py:31
  16.2 0.7 copy-start.3
  16.2 78.0 %copy-start.1 = (f32[4,2,32,512]{3,2,1,0:T(8,128)S(1)}, f32[4,2,32,512]{3,2,1,0:T(8,128)}, u32[]{:S(2)}) copy-start(f32[4,2,32,512]{3,2,1,0:T(8,128)} %param.9) | copy-start | bytes 1572868
  16.2 78.0 %copy-start.2 = (f32[4,2,32,512]{3,2,1,0:T(8,128)S(1)}, f32[4,2,32,512]{3,2,1,0:T(8,128)}, u32[]{:S(2)}) copy-start(f32[4,2,32,512]{3,2,1,0:T(8,128)} %param.10) | copy-start | bytes 1572868
  96.5 5.4 %copy-start = (f32[1,4,32,4096]{3,2,1,0:T(8,128)S(1)}, f32[1,4,32,4096]{3,2,1,0:T(8,128)}, u32[]{:S(2)}) copy-start(f32[1,4,32,4096]{3,2,1,0:T(8,128)} %param.8) | copy-start | bytes 6291460
  97.6 30.8 %all-to-all-start = ((bf16[8,4,32,512]{3,2,1,0:T(8,128)(2,1)}), bf16[8,4,32,512]{3,2,1,0:T(8,128)(2,1)S(1)}, u32[]{:S(2)}, u32[]{:S(2)}) async-start(bf16[8,4,32,512]{3,2,1,0:T(8,128)(2,1)} %broadcast_select_fusion), calls=%async_computation.1 | async-start | bytes 2097152 | tf_op jit(solution)/shard_map/all_to_all | solution.py:48
Sparse Core Ops, SparseCore 0:
  16.3 38.7 reduce-scatter.1
where the time goes:
time: 137 us; the launch traced here: 136 us
  waiting for transfers between devices  61.7 us (45%)
  blocking collectives  37.9 us (28%)
  other arithmetic  14.6 us (11%)
  between operations  14.1 us (10%)
  starting transfers between devices  4.26 us (3%)
  local copies, waits for them, and re-layouts  3.82 us (3%)
    reduce_scatter x1, waiting for transfers between devices, on_device(): lax.psum_scatter(terms.astype(jnp.bfloat16), 'path', scatter_dimension=3,...  38.2 us
    psum x1, blocking collectives, on_device(): total_sq = lax.psum(local_sq, ('path', 'fsdp'))  37.9 us
    all_to_all x1, waiting for transfers between devices, on_device(): lax.all_to_all(outgoing, 'path', split_axis=0, concat_axis=3, tiled=True)  23.5 us
    all_to_all x1, starting transfers between devices, on_device(): lax.all_to_all(outgoing, 'path', split_axis=0, concat_axis=3, tiled=True)  4.22 us
    sub x1, other arithmetic, on_device(): corrected - own_live[:, None, None] * (sent.astype(jnp.float32) / own_wei...  3.07 us
  transfers between devices with their start and end apart: 2, of which 2 were waited for; matrix products, arithmetic and copies ran while one was open for 2% of the time, Pallas kernels for 0%

commit v1 on v0

--- a/solution.py
+++ b/solution.py
@@ -45,7 +45,10 @@
     )
     narrow = params_next.astype(jnp.bfloat16)
     outgoing = jnp.where((routes == 1)[:, :, None, None], narrow[None, :, 1], narrow[None, :, 0])
-    returned = lax.all_to_all(outgoing, "path", split_axis=0, concat_axis=3, tiled=True)
+    returned = jnp.concatenate(
+        lax.all_to_all(jnp.stack(jnp.split(outgoing, lax.axis_size("path"), axis=0)), "path", 0, 0),
+        axis=3,
+    )
     return (feedback_next[None], momentum_next, params_next, returned)
 
 

time: 137 us -> 141 us (1.029)
  local copies, waits for them, and re-layouts: 3.82 us -> 9.13 us
    unnamed x8 -> x15, local copies, waits for them, and re-layouts: 0.66 us -> 5.31 us
where the time goes in v1:
time: 141 us
  waiting for transfers between devices  61.7 us (44%)
  blocking collectives  37.9 us (27%)
  between operations  14.1 us (10%)
  other arithmetic  13.7 us (10%)
  local copies, waits for them, and re-layouts  9.13 us (6%)
  starting transfers between devices  4.26 us (3%)
    reduce_scatter x1, waiting for transfers between devices, on_device(): lax.psum_scatter(terms.astype(jnp.bfloat16), 'path', scatter_dimension=3,...  38.2 us
    psum x1, blocking collectives, on_device(): total_sq = lax.psum(local_sq, ('path', 'fsdp'))  37.9 us
    all_to_all x1, waiting for transfers between devices, on_device(): lax.all_to_all(jnp.stack(jnp.split(outgoing, lax.axis_size('path'), axis=...  23.5 us
    unnamed x15, local copies, waits for them, and re-layouts  5.31 us
    all_to_all x1, starting transfers between devices, on_device(): lax.all_to_all(jnp.stack(jnp.split(outgoing, lax.axis_size('path'), axis=...  4.22 us
    sub x1, other arithmetic, on_device(): corrected - own_live[:, None, None] * (sent.astype(jnp.float32) / own_wei...  3.07 us
  transfers between devices with their start and end apart: 2, of which 2 were waited for; matrix products, arithmetic and copies ran while one was open for 2% of the time, Pallas kernels for 0%

profile of v1, /device:TPU:0, one launch (start us, length us, event | category | flops | bytes accessed | tf_op | source)
XLA Modules:
  0.0 140.7 jit_solution(3726895523455588675)
XLA Ops:
  7.2 0.0 reduce-scatter.2.cloned.1.call-start
  7.2 0.8 slice_bitcast_fusion.11
  8.0 0.7 convert_element_type.55
  8.7 0.9 select_reduce_fusion
  9.6 0.7 convert_divide_fusion
  10.3 0.9 dynamic-slice_reduce_fusion
  11.1 0.8 subtract_convert_fusion
  11.9 0.2 dynamic-slice_reduce_fusion.1
  12.1 0.1 fusion.17
  12.2 2.3 %fusion.3 = f32[4,32,4096]{2,1,0:T(8,128)S(1)} fusion(f32[1,4,32,4096]{3,2,1,0:T(8,128)} %param.8, bf16[1,4,32,4096]{3,2,1,0:T(8,128)(2,1)} %param.7, f32[4]{0:T(128)S(1)} %get-tuple-element.13, pred[4]{0:T(512)(128)(4,1)S(1)} %broadcast_compare_fusion.2), kind=kLoop, calls=%fused_computation.8 | loop fusion | flops 3145728 | bytes 5242900 | tf_op jit(solution)/shard_map/convert_element_type | solution.py:27
  14.5 1.7 %multiply_convert_fusion = bf16[4,2,32,4096]{3,2,1,0:T(8,128)(2,1)} fusion(f32[4,32,4096]{2,1,0:T(8,128)S(1)} %fusion.3, f32[4,2]{1,0:T(4,128)S(1)} %fusion.17), kind=kLoop, calls=%fused_computation | loop fusion | flops 2097152 | bytes 4194336 | tf_op jit(solution)/shard_map/convert_element_type | solution.py:32
  16.2 0.0 copy-start.3
  16.2 0.0 copy-start.1
  16.2 0.0 copy-start.2
  16.2 0.0 reduce-scatter.2.cloned.1.call-update
  16.2 0.6 copy-done.3
  16.9 0.1 copy.37
  17.0 38.2 %reduce-scatter.2.cloned.1.call-done = bf16[4,2,32,512]{3,2,1,0:T(8,128)(2,1)} async-done(((bf16[4,2,32,4096]{3,2,1,0:T(8,128)(2,1)}), bf16[4,2,32,512]{3,2,1,0:T(8,128)(2,1)}) %reduce-scatter.2.cloned.1.call-update) | async-done | bytes 262160 | tf_op jit(solution)/shard_map/reduce_scatter | solution.py:31
  55.1 1.1 fusion.8
  56.2 0.1 copy.38
  56.3 37.9 %psum.7 = f32[4,2]{1,0:T(4,128)S(1)} all-reduce(f32[4,2]{1,0:T(4,128)S(1)} %fusion.8), channel_id=1, replica_groups=mesh['path'=8,'fsdp'=4] {'path','fsdp'}, use_global_device_ids=true, to_apply=%region_3.4 | all-reduce | flops 8 | bytes 64 | tf_op jit(solution)/shard_map/psum | solution.py:35
  94.2 0.0 copy-done.1
  94.2 0.0 copy-done.2
  94.2 2.2 %fusion.18 = (bf16[4,2,32,512]{3,2,1,0:T(8,128)(2,1)S(1)}, f32[4,2,32,512]{3,2,1,0:T(8,128)}, f32[4,2,32,512]{3,2,1,0:T(8,128)}) fusion(f32[4,2,32,512]{3,2,1,0:T(8,128)S(1)} %copy-done.1, bf16[4,2,32,512]{3,2,1,0:T(8,128)(2,1)} %reduce-scatter.2.cloned.1.call-done, f32[4,2]{1,0:T(4,128)S(1)} %multiply_minimum_fusion, pred[4,2]{1,0:T(4,128)(4,1)S(1)} %copy.37, ...), kind=kLoop, calls=%fused_computation.50 | loop fusion | flops 1441792 | bytes 2621480 | tf_op jit(solution)/shard_map/convert_element_type | solution.py:46
  96.5 0.1 broadcast_select_fusion
  96.6 0.0 copy-start
  96.7 0.7 fusion.16
  97.3 0.7 fusion.15
  98.0 0.7 fusion.14
  98.6 0.7 fusion.13
  99.3 0.7 fusion.12
  100.0 0.7 fusion.11
  100.6 0.7 fusion.10
  101.3 0.7 fusion.9
  102.0 4.2 %all-to-all-start = ((bf16[8,1,4,32,512]{4,3,2,1,0:T(8,128)(2,1)}), bf16[8,1,4,32,512]{4,3,2,1,0:T(8,128)(2,1)S(1)}, u32[]{:S(2)}, u32[]{:S(2)}) async-start(bf16[8,1,4,32,512]{4,3,2,1,0:T(8,128)(2,1)} %fusion.9), calls=%async_computation.1 | async-start | bytes 2097152 | tf_op jit(solution)/shard_map/all_to_all | solution.py:49
  106.2 0.0 copy-done
  106.2 3.1 %multiply_subtract_fusion = f32[1,4,32,4096]{3,2,1,0:T(8,128)} fusion(f32[1,4,32,4096]{3,2,1,0:T(8,128)S(1)} %copy-done, bf16[1,4,32,4096]{3,2,1,0:T(8,128)(2,1)} %param.7, f32[4]{0:T(128)S(1)} %get-tuple-element.13, f32[4]{0:T(128)S(1)} %get-tuple-element.14, pred[4]{0:T(512)(128)(4,1)S(1)} %broadcast_compare_fusion.2), kind=kLoop, calls=%fused_computation.3 | loop fusion | flops 4718592 | bytes 5242916 | tf_op jit(solution)/shard_map/sub | solution.py:26
  109.3 23.5 %all-to-all-done = bf16[8,1,4,32,512]{4,3,2,1,0:T(8,128)(2,1)S(1)} async-done(((bf16[8,1,4,32,512]{4,3,2,1,0:T(8,128)(2,1)}), bf16[8,1,4,32,512]{4,3,2,1,0:T(8,128)(2,1)S(1)}, u32[]{:S(2)}, u32[]{:S(2)}) %all-to-all-start) | async-done | bytes 1048608 | tf_op jit(solution)/shard_map/all_to_all | solution.py:49
  132.8 1.1 copy.40
  (4 shorter events, 0.0 us)
Async XLA Ops:
  7.2 48.0 %reduce-scatter.2.cloned.1.call-start = ((), (), s32[]{:S(2)}) async-start(), calls=%async_computation.2 | async-start | bytes 2359296 | tf_op jit(solution)/shard_map/reduce_scatter | solution.py:31
  16.2 0.7 copy-start.3
  16.2 78.0 %copy-start.1 = (f32[4,2,32,512]{3,2,1,0:T(8,128)S(1)}, f32[4,2,32,512]{3,2,1,0:T(8,128)}, u32[]{:S(2)}) copy-start(f32[4,2,32,512]{3,2,1,0:T(8,128)} %param.9) | copy-start | bytes 1572868
  16.2 78.0 %copy-start.2 = (f32[4,2,32,512]{3,2,1,0:T(8,128)S(1)}, f32[4,2,32,512]{3,2,1,0:T(8,128)}, u32[]{:S(2)}) copy-start(f32[4,2,32,512]{3,2,1,0:T(8,128)} %param.10) | copy-start | bytes 1572868
  96.6 9.6 %copy-start = (f32[1,4,32,4096]{3,2,1,0:T(8,128)S(1)}, f32[1,4,32,4096]{3,2,1,0:T(8,128)}, u32[]{:S(2)}) copy-start(f32[1,4,32,4096]{3,2,1,0:T(8,128)} %param.8) | copy-start | bytes 6291460
  102.0 30.8 %all-to-all-start = ((bf16[8,1,4,32,512]{4,3,2,1,0:T(8,128)(2,1)}), bf16[8,1,4,32,512]{4,3,2,1,0:T(8,128)(2,1)S(1)}, u32[]{:S(2)}, u32[]{:S(2)}) async-start(bf16[8,1,4,32,512]{4,3,2,1,0:T(8,128)(2,1)} %fusion.9), calls=%async_computation.1 | async-start | bytes 2097152 | tf_op jit(solution)/shard_map/all_to_all | solution.py:49
Sparse Core Ops, SparseCore 0:
  16.3 38.7 reduce-scatter.1
